TPU v7x, 512 devices: a whole 4x4x16 slice. The times are simulated.
512 devices in a mesh: tile: 32 (over y, x, core), fsdp: 16 (over z).
Axes of the slice: x: 4, y: 4, z: 16, core: 2. Of those that a mesh axis runs over, the one named last changes fastest.
Arguments:
- images: bfloat16 [16, 32, 8, 128, 320], P('fsdp', 'tile'), may hold values from -80 to 80
- tile_rows: int32 [16, 32], P('fsdp', 'tile'), may hold values from 1 to 8, 160 in all within a row
- cotangent: bfloat16 [16, 32, 8, 128, 320], P('fsdp', 'tile'), may hold values from -6 to 6
- master_weight: float32 [2880, 320], P('fsdp'), may hold values from -0.109375 to 0.109375
- norm_gain: float32 [320], replicated, may hold values from 0.5 to 1.5
- norm_bias: float32 [320], replicated, may hold values from -3 to 3
- first_moment: float32 [2880, 320], P('fsdp'), may hold values from -6 to 6
- second_moment: float32 [2880, 320], P('fsdp'), may hold values from 0.5 to 4
Outputs:
- activation: bfloat16 [16, 32, 8, 128, 320], P('fsdp', 'tile')
- image_grad: bfloat16 [16, 32, 8, 128, 320], P('fsdp', 'tile')
- weight_grad: float32 [2880, 320], P('fsdp')
- new_weight: float32 [2880, 320], P('fsdp')
- new_first: float32 [2880, 320], P('fsdp')
- new_second: float32 [2880, 320], P('fsdp')
- gain_grad: float32 [320], replicated
- bias_grad: float32 [320], replicated
Inputs may be any that keep to these rules, and one draw needn't show every extreme that they name: `tile_rows`: in each frame the 32 counts sum to 160 and the largest is exactly 8.
All inputs are finite; a program needn't handle non-finite values. No bound on the sum of `tile_rows` on one device may be relied on, other than what follows from the above.
Results may differ from a plain program's by a relative error of at most 0.027.
Values may be sent and summed in bfloat16 or wider, within the bound.
No kernel may reach another device: no remote copies, remote signals or barrier semaphores. Data moves between devices by JAX's collectives and lax.ppermute only.
A program may use at most 64 MiB of HBM per device.

v0:
```python
import jax
import jax.numpy as jnp
from jax import lax
from jax.sharding import PartitionSpec as P

GROUPS = 32
ROWS_MEAN = 5


def extended(cells, sides, width):
    for axis, dim in sides:
        count = lax.axis_size(axis)
        ends = count - 1
        head = lax.slice_in_dim(cells, 0, width, axis=dim)
        tail = lax.slice_in_dim(cells, cells.shape[dim] - width, cells.shape[dim], axis=dim)
        cells = jnp.concatenate(
            [
                lax.ppermute(tail, axis, [(i, (i + 1) % count) for i in range(ends)]),
                cells,
                lax.ppermute(head, axis, [((i + 1) % count, i) for i in range(ends)]),
            ],
            axis=dim,
        )
    return cells


def edge_pair(source, live_count):
    first_row = source[0:1]
    last_row = lax.dynamic_slice_in_dim(source, live_count - 1, 1, 0)
    return jnp.concatenate([first_row, last_row], axis=0)


def framed(source, beside_all, live_count):
    slot_count = source.shape[0]
    zero_row = jnp.zeros_like(source[0:1])
    stacked = jnp.concatenate([beside_all[0:1], source, zero_row], axis=0)
    marker = (jnp.arange(slot_count + 2) == live_count + 1)[:, None, None]
    stacked = jnp.where(marker, beside_all[3:4], stacked)
    return jnp.pad(stacked, ((0, 0), (1, 1), (0, 0)))


def patches_of(padded, slot_count, cell_cols):
    pieces = [
        padded[row_step : row_step + slot_count, col_step : col_step + cell_cols, :]
        for row_step in range(3)
        for col_step in range(3)
    ]
    return jnp.concatenate(pieces, axis=-1).reshape(slot_count * cell_cols, -1)


def local(
    images, tile_rows, cotangent, master_weight, norm_gain, norm_bias, first_moment, second_moment
):
    slot_count, cell_cols, channels = (images.shape[2], images.shape[3], images.shape[4])
    per_group = channels // GROUPS
    tile_count = lax.axis_size("tile")
    shards = lax.axis_size("fsdp")
    population = jnp.float32(ROWS_MEAN * tile_count * cell_cols * per_group)
    live_count = tile_rows[0, 0]
    live_rows = jnp.arange(slot_count) < live_count
    cell_mask = jnp.repeat(live_rows, cell_cols).astype(jnp.float32)[:, None]

    def grouped(values):
        return jnp.sum(values.reshape(-1, GROUPS, per_group), axis=(0, 2))

    def spread(stat):
        return jnp.repeat(stat, per_group)

    source = jnp.where(live_rows[:, None, None], images[0, 0], jnp.zeros((), jnp.bfloat16))
    beside_all = extended(edge_pair(source, live_count), (("tile", 0),), 1)
    columns = patches_of(framed(source, beside_all, live_count), slot_count, cell_cols)
    gathered = lax.all_gather(master_weight.astype(jnp.bfloat16), "fsdp", axis=0, tiled=True)
    mixed = jnp.dot(columns, gathered, preferred_element_type=jnp.float32)
    group_mean = lax.psum(grouped(mixed * cell_mask), "tile") / population
    centered = (mixed - spread(group_mean)) * cell_mask
    variance = lax.psum(grouped(centered * centered), "tile") / population
    inverse = lax.rsqrt(variance + 1e-05)
    normed = (mixed - spread(group_mean)) * spread(inverse)
    shifted = normed * norm_gain + norm_bias
    gate_value = jax.nn.sigmoid(shifted)
    activation = (shifted * gate_value * cell_mask).astype(jnp.bfloat16).reshape(images.shape)
    upstream = cotangent[0, 0].reshape(-1, channels).astype(jnp.float32) * cell_mask
    dshift = upstream * gate_value * (1.0 + shifted * (1.0 - gate_value))
    scaled = dshift * norm_gain
    delta_sum, cross_sum = lax.psum((grouped(scaled), grouped(scaled * normed)), "tile")
    gain_total, bias_total = lax.psum(
        (jnp.sum(dshift * normed, axis=0), jnp.sum(dshift, axis=0)), ("tile", "fsdp")
    )
    norm_scale = jnp.float32(shards * ROWS_MEAN * tile_count * cell_cols) ** (-0.5)
    pre_grad = spread(inverse) * (
        scaled - spread(delta_sum / population) - normed * spread(cross_sum / population)
    )
    pre_grad = (pre_grad * cell_mask).astype(jnp.bfloat16)
    grad_field = pre_grad.reshape(slot_count, cell_cols, channels)
    grad_around = extended(edge_pair(grad_field, live_count), (("tile", 0),), 1)
    grad_columns = patches_of(framed(grad_field, grad_around, live_count), slot_count, cell_cols)
    flipped = (
        gathered.reshape(9, channels, channels)[::-1]
        .transpose(0, 2, 1)
        .reshape(9 * channels, channels)
    )
    image_grad = (
        (jnp.dot(grad_columns, flipped, preferred_element_type=jnp.float32) * cell_mask)
        .astype(jnp.bfloat16)
        .reshape(images.shape)
    )
    full_grad = lax.psum(
        lax.dot_general(
            columns, pre_grad, (((0,), (0,)), ((), ())), preferred_element_type=jnp.float32
        ).astype(jnp.bfloat16),
        "tile",
    )
    grad_shard = lax.psum_scatter(full_grad, "fsdp", scatter_dimension=0, tiled=True).astype(
        jnp.float32
    )
    weight_grad = grad_shard * norm_scale
    new_first = 0.9 * first_moment + 0.1 * weight_grad
    new_second = 0.999 * second_moment + 0.001 * weight_grad * weight_grad
    first_fix = new_first / (1.0 - 0.9**10)
    second_fix = new_second / (1.0 - 0.999**10)
    new_weight = master_weight - 0.01 * first_fix / (jnp.sqrt(second_fix) + 1e-08)
    return (
        activation,
        image_grad,
        weight_grad,
        new_weight,
        new_first,
        new_second,
        gain_total * norm_scale,
        bias_total * norm_scale,
    )


def solution(mesh):
    placed = (
        P("fsdp", "tile", None, None, None),
        P("fsdp", "tile"),
        P("fsdp", "tile", None, None, None),
        P("fsdp", None),
        P(),
        P(),
        P("fsdp", None),
        P("fsdp", None),
    )
    return jax.shard_map(
        local,
        mesh=mesh,
        in_specs=placed,
        out_specs=(
            P("fsdp", "tile", None, None, None),
            P("fsdp", "tile", None, None, None),
            P("fsdp", None),
            P("fsdp", None),
            P("fsdp", None),
            P("fsdp", None),
            P(),
            P(),
        ),
        check_vma=False,
    )
```

profile of v0, /device:TPU:1, one launch (start us, length us, event | category | flops | bytes accessed | tf_op | source)
XLA Modules:
  0.0 609.0 jit_solution(12582963821743056391)
XLA Ops:
  7.2 1.7 convert_bitcast_fusion
  9.7 1.2 bitcast_select_fusion
  10.9 8.8 %collective-permute-start = (bf16[1,128,320]{1,2,0:T(8,128)(2,1)S(1)}, bf16[1,128,320]{1,2,0:T(8,128)(2,1)S(1)}, u32[]{:S(2)}, u32[]{:S(2)}) collective-permute-start(bf16[1,128,320]{1,2,0:T(8,128)(2,1)S(1)} %get-tuple-element.46), channel_id=1, source_target_pairs={{16,0},{32,16},{48,32},{64,48},{80,64},{96,80},{112,96},{128,112},... | collective-permute-start | bytes 245768 | tf_op jit(solution)/shard_map/ppermute | solution.py:20
  19.7 1.9 collective-permute-start.1
  21.6 1.5 copy.30
  23.2 1.3 dynamic-slice.4
  25.4 1.1 fusion.5
  26.5 1.0 slice_dynamic-update-slice_fusion.5
  27.5 1.1 fusion.6
  28.6 1.1 fusion.7
  29.7 1.0 slice_dynamic-update-slice_fusion.4
  30.7 1.1 fusion.8
  31.8 1.1 fusion.9
  32.9 1.0 slice_dynamic-update-slice_fusion.3
  33.8 1.1 fusion.10
  34.9 8.4 %copy.29 = bf16[8,128,2880]{2,1,0:T(8,128)(2,1)} copy(bf16[8,128,2880]{1,2,0:T(8,128)(2,1)} %fusion.10) | data formatting | bytes 11796480 | tf_op jit(solution)/shard_map/concatenate | solution.py:48
  43.4 37.7 %all-gather.3.cloned.1.call-done = bf16[16,180,320]{2,1,0:T(8,128)(2,1)} async-done(((bf16[1,180,320]{2,1,0:T(8,128)(2,1)}), bf16[16,180,320]{2,1,0:T(8,128)(2,1)}) %all-gather.3.cloned.1.call-update) | async-done | bytes 1843216 | tf_op jit(solution)/shard_map/all_gather | solution.py:72
  81.1 2.8 reshape.78
  83.8 5.1 multiply_reduce_fusion.3
  89.1 71.5 %psum.49 = f32[32]{0:T(128)S(1)} all-reduce(f32[32]{0:T(128)S(1)} %reduce_sum.67), channel_id=1, replica_groups=mesh['tile'=32,'fsdp'=16] {'tile'}, use_global_device_ids=true, to_apply=%region_2.3 | all-reduce | flops 32 | bytes 256 | tf_op jit(solution)/shard_map/psum | solution.py:74
  161.4 62.7 %psum.50 = f32[32]{0:T(128)S(1)} all-reduce(f32[32]{0:T(128)S(1)} %reduce_sum.73), channel_id=1, replica_groups=mesh['tile'=32,'fsdp'=16] {'tile'}, use_global_device_ids=true, to_apply=%region_5.6 | all-reduce | flops 32 | bytes 256 | tf_op jit(solution)/shard_map/psum | solution.py:76
  224.3 3.5 multiply_reduce_fusion
  228.2 62.9 %all-reduce.5 = (f32[32]{0:T(128)S(1)}, f32[32]{0:T(128)S(1)}) all-reduce(f32[32]{0:T(128)S(1)} %reduce_sum.93, f32[32]{0:T(128)S(1)} %reduce_sum.90), channel_id=1, replica_groups=mesh['tile'=32,'fsdp'=16] {'tile'}, use_global_device_ids=true, to_apply=%region_11.12 | all-reduce | flops 64 | bytes 512 | tf_op jit(solution)/shard_map/psum | solution.py:85
  292.3 7.4 %convolution_convert_fusion = bf16[2880,320]{1,0:T(8,128)(2,1)} fusion(bf16[1024,2880]{1,0:T(8,128)(2,1)} %bitcast.60, bf16[1024,320]{0,1:T(8,128)(2,1)S(1)} %multiply_convert_fusion), kind=kOutput, calls=%fused_computation | convolution fusion | flops 1888358400 | bytes 8396800 | tf_op jit(solution)/shard_map/dot_general | solution.py:108
  300.5 33.6 %fusion = bf16[192,320]{1,0:T(8,128)(2,1)S(1)} fusion(bf16[2880,320]{1,0:T(8,128)(2,1)} %convolution_convert_fusion), kind=kCustom, calls=%all-reduce-scatter | all-reduce-scatter fusion | flops 983041 | bytes 1968128
  334.1 2.7 collective-permute-start.4
  337.5 5.1 collective-permute-start.3
  342.6 5.2 collective-permute-start.2
  347.8 100.6 %all-reduce.4 = (f32[320]{0:T(512)S(1)}, f32[320]{0:T(512)S(1)}) all-reduce(f32[320]{0:T(512)S(1)} %get-tuple-element.32, f32[320]{0:T(512)S(1)} %get-tuple-element.35), channel_id=1, replica_groups=mesh['tile'=32,'fsdp'=16] {'tile','fsdp'}, use_global_device_ids=true, to_apply=%region_15.16 | all-reduce | flops 640 | bytes 5120 | tf_op jit(solution)/shard_map/psum | solution.py:86
  449.0 2.2 reshape.73
  451.2 1.8 reverse_bitcast_fusion
  453.1 2.5 copy.34
  455.6 1.2 copy.38
  456.8 0.9 copy.35
  457.9 1.1 fusion.11
  459.0 1.0 slice_dynamic-update-slice_fusion.2
  460.0 1.1 fusion.12
  461.2 1.1 fusion.13
  462.3 1.0 slice_dynamic-update-slice_fusion.1
  463.3 1.1 fusion.14
  464.3 1.1 fusion.15
  465.4 1.0 slice_dynamic-update-slice_fusion
  466.4 1.1 fusion.16
  467.5 8.6 %copy.33 = bf16[8,128,2880]{2,1,0:T(8,128)(2,1)} copy(bf16[8,128,2880]{1,2,0:T(8,128)(2,1)} %fusion.16) | data formatting | bytes 11796480 | tf_op jit(solution)/shard_map/concatenate | solution.py:48
  477.7 4.9 fusion.4
  482.8 0.9 copy.36
  483.8 116.3 %all-reduce.8.cloned.1.call-done = bf16[180,320]{1,0:T(8,128)(2,1)} async-done(((bf16[180,320]{1,0:T(8,128)(2,1)}), bf16[180,320]{1,0:T(8,128)(2,1)}) %all-reduce.8.cloned.1.call-update) | async-done | bytes 115216 | tf_op jit(solution)/shard_map/psum | solution.py:107
  600.1 2.0 divide_subtract_fusion
  (62 shorter events, 7.3 us)
Async XLA Ops:
  7.2 14.4 %copy-start.3 = (bf16[1,1,8,128,320]{3,4,2,1,0:T(8,128)(2,1)S(1)}, bf16[1,1,8,128,320]{3,4,2,1,0:T(8,128)(2,1)}, u32[]{:S(2)}) copy-start(bf16[1,1,8,128,320]{3,4,2,1,0:T(8,128)(2,1)} %param.10) | copy-start | bytes 1966084
  7.2 73.9 %all-gather.3.cloned.1.call-start = ((), (), s32[]{:S(2)}) async-start(), calls=%async_computation.1 | async-start | bytes 2402304 | tf_op jit(solution)/shard_map/all_gather | solution.py:72
  8.9 591.2 %all-reduce.8.cloned.1.call-start = ((), (), s32[]{:S(2)}) async-start(), calls=%async_computation | async-start | bytes 282624 | tf_op jit(solution)/shard_map/psum | solution.py:107
  10.9 14.3 %collective-permute-start = (bf16[1,128,320]{1,2,0:T(8,128)(2,1)S(1)}, bf16[1,128,320]{1,2,0:T(8,128)(2,1)S(1)}, u32[]{:S(2)}, u32[]{:S(2)}) collective-permute-start(bf16[1,128,320]{1,2,0:T(8,128)(2,1)S(1)} %get-tuple-element.46), channel_id=1, source_target_pairs={{16,0},{32,16},{48,32},{64,48},{80,64},{96,80},{112,96},{128,112},... | collective-permute-start | bytes 245768 | tf_op jit(solution)/shard_map/ppermute | solution.py:20
  19.7 5.5 collective-permute-start.1
  83.8 140.5 %copy-start.6 = (f32[320]{0:T(512)S(1)}, f32[320]{0:T(512)}, u32[]{:S(2)}) copy-start(f32[320]{0:T(512)} %param.12) | copy-start | bytes 3844
  83.8 140.5 %copy-start.7 = (f32[320]{0:T(512)S(1)}, f32[320]{0:T(512)}, u32[]{:S(2)}) copy-start(f32[320]{0:T(512)} %param.13) | copy-start | bytes 3844
  299.8 149.2 %copy-start = (bf16[16,180,320]{2,1,0:T(8,128)(2,1)S(1)}, bf16[16,180,320]{2,1,0:T(8,128)(2,1)}, u32[]{:S(2)}) copy-start(bf16[16,180,320]{2,1,0:T(8,128)(2,1)} %all-gather.3.cloned.1.call-done) | copy-start | bytes 5529604
  334.1 141.9 %collective-permute-start.4 = (bf16[180,320]{1,0:T(8,128)(2,1)S(1)}, bf16[180,320]{1,0:T(8,128)(2,1)S(1)}, u32[]{:S(2)}, u32[]{:S(2)}) collective-permute-start(bf16[180,320]{1,0:T(8,128)(2,1)S(1)} %slice.98), channel_id=1, source_target_pairs={{0,1},{1,2},{2,3},{3,4},{4,5},{5,6},{6,7},{7,8},{8,9},{9,10},{10,1... | collective-permute-start | bytes 345608
  337.5 120.2 %collective-permute-start.3 = (bf16[1,128,320]{1,2,0:T(8,128)(2,1)}, bf16[1,128,320]{1,2,0:T(8,128)(2,1)S(1)}, u32[]{:S(2)}, u32[]{:S(2)}) collective-permute-start(bf16[1,128,320]{1,2,0:T(8,128)(2,1)} %constant_dynamic-slice_fusion.1), channel_id=1, source_target_pairs={{0,16},{16,32},{32,48},{48,64},{64,80},{80,96},{96,112},{112,128},... | collective-permute-start | bytes 245768 | tf_op jit(solution)/shard_map/ppermute | solution.py:18
  342.6 115.2 %collective-permute-start.2 = (bf16[1,128,320]{1,2,0:T(8,128)(2,1)}, bf16[1,128,320]{1,2,0:T(8,128)(2,1)S(1)}, u32[]{:S(2)}, u32[]{:S(2)}) collective-permute-start(bf16[1,128,320]{1,2,0:T(8,128)(2,1)} %slice_bitcast_fusion), channel_id=1, source_target_pairs={{16,0},{32,16},{48,32},{64,48},{80,64},{96,80},{112,96},{128,112},... | collective-permute-start | bytes 245768 | tf_op jit(solution)/shard_map/ppermute | solution.py:20
  467.5 10.2 %copy-start.1 = (bf16[9,320,320]{2,1,0:T(8,128)(2,1)S(1)}, bf16[9,320,320]{2,1,0:T(8,128)(2,1)}, u32[]{:S(2)}) copy-start(bf16[9,320,320]{2,1,0:T(8,128)(2,1)} %copy.34) | copy-start | bytes 5529604
  482.6 117.5 %copy-start.2 = (f32[180,320]{1,0:T(8,128)S(1)}, f32[180,320]{1,0:T(8,128)}, u32[]{:S(2)}) copy-start(f32[180,320]{1,0:T(8,128)} %param.11) | copy-start | bytes 691204
  482.7 117.4 %copy-start.4 = (f32[180,320]{1,0:T(8,128)S(1)}, f32[180,320]{1,0:T(8,128)}, u32[]{:S(2)}) copy-start(f32[180,320]{1,0:T(8,128)} %param.14) | copy-start | bytes 691204
  482.7 117.4 %copy-start.5 = (f32[180,320]{1,0:T(8,128)S(1)}, f32[180,320]{1,0:T(8,128)}, u32[]{:S(2)}) copy-start(f32[180,320]{1,0:T(8,128)} %param.15) | copy-start | bytes 691204
Sparse Core Ops, SparseCore 0:
  10.7 70.3 all-gather.2
  477.8 122.2 all-reduce.7
where the time goes:
time: 610 us; the launch traced here: 609 us
  blocking collectives  331 us (54%)
  waiting for transfers between devices  154 us (25%)
  local copies, waits for them, and re-layouts  55.7 us (9%)
  starting transfers between devices  23.8 us (4%)
  matrix products  17.4 us (3%)
  between operations  15.7 us (3%)
  other arithmetic  11.1 us (2%)
    psum x1, waiting for transfers between devices, local(): lax.psum(lax.dot_general(columns, pre_grad, (((0,), (0,)), ((), ())), pre...  116 us
    psum x1, blocking collectives, local(): lax.psum((jnp.sum(dshift * normed, axis=0), jnp.sum(dshift, axis=0)), ('t...  101 us
    psum x1, blocking collectives, local(): group_mean = lax.psum(grouped(mixed * cell_mask), 'tile') / population  71.5 us
    psum x1, blocking collectives, local(): lax.psum((grouped(scaled), grouped(scaled * normed)), 'tile')  62.9 us
    psum x1, blocking collectives, local(): variance = lax.psum(grouped(centered * centered), 'tile') / population  62.7 us
    all_gather x1, waiting for transfers between devices, local(): lax.all_gather(master_weight.astype(jnp.bfloat16), 'fsdp', axis=0, tiled=...  37.7 us
    unnamed x1, blocking collectives  33.6 us
    unnamed x41, local copies, waits for them, and re-layouts  25.8 us
  transfers between devices with their start and end apart: 7, of which 2 were waited for; matrix products, arithmetic and copies ran while one was open for 9% of the time, Pallas kernels for 0%

commit v1 on v0

--- a/solution.py
+++ b/solution.py
@@ -84,7 +84,7 @@
     scaled = dshift * norm_gain
     delta_sum, cross_sum = lax.psum((grouped(scaled), grouped(scaled * normed)), "tile")
     gain_total, bias_total = lax.psum(
-        (jnp.sum(dshift * normed, axis=0), jnp.sum(dshift, axis=0)), ("tile", "fsdp")
+        lax.psum((jnp.sum(dshift * normed, axis=0), jnp.sum(dshift, axis=0)), "fsdp"), "tile"
     )
     norm_scale = jnp.float32(shards * ROWS_MEAN * tile_count * cell_cols) ** (-0.5)
     pre_grad = spread(inverse) * (

time: 610 us -> 538 us (0.88)
  blocking collectives: 331 us -> 261 us
    psum x1, blocking collectives: 101 us -> 22.8 us  [local(): lax.psum((jnp.sum(dshift * normed, axis=0), jnp.sum(dshift, axis=0)), 'fs...]
    psum x1, blocking collectives: 62.9 us -> 70.8 us  [local(): lax.psum((grouped(scaled), grouped(scaled * normed)), 'tile')]
  transfers between devices with their start and end apart: 7 -> 7, of which waited for: 2 -> 2; matrix products, arithmetic and copies ran while one was open for 9% -> 11% of each run, Pallas kernels for 0% -> 0%
where the time goes in v1:
time: 538 us; the launch traced here: 537 us
  blocking collectives  261 us (49%)
  waiting for transfers between devices  153 us (28%)
  local copies, waits for them, and re-layouts  55.7 us (10%)
  starting transfers between devices  23.3 us (4%)
  matrix products  17.4 us (3%)
  between operations  15.7 us (3%)
  other arithmetic  11.1 us (2%)
    psum x1, waiting for transfers between devices, local(): lax.psum(lax.dot_general(columns, pre_grad, (((0,), (0,)), ((), ())), pre...  115 us
    psum x1, blocking collectives, local(): group_mean = lax.psum(grouped(mixed * cell_mask), 'tile') / population  71.5 us
    psum x1, blocking collectives, local(): lax.psum((grouped(scaled), grouped(scaled * normed)), 'tile')  70.8 us
    psum x1, blocking collectives, local(): variance = lax.psum(grouped(centered * centered), 'tile') / population  62.7 us
    all_gather x1, waiting for transfers between devices, local(): lax.all_gather(master_weight.astype(jnp.bfloat16), 'fsdp', axis=0, tiled=...  37.7 us
    unnamed x1, blocking collectives  32.9 us
    unnamed x41, local copies, waits for them, and re-layouts  25.8 us
    psum x1, blocking collectives, local(): lax.psum((jnp.sum(dshift * normed, axis=0), jnp.sum(dshift, axis=0)), 'fs...  22.8 us
  transfers between devices with their start and end apart: 7, of which 2 were waited for; matrix products, arithmetic and copies ran while one was open for 11% of the time, Pallas kernels for 0%

profile of v1, /device:TPU:1, one launch (start us, length us, event | category | flops | bytes accessed | tf_op | source)
XLA Modules:
  0.0 537.0 jit_solution(8263171554684661322)
XLA Ops:
  7.2 1.7 convert_bitcast_fusion
  9.7 1.2 bitcast_select_fusion
  10.9 8.8 %collective-permute-start = (bf16[1,128,320]{1,2,0:T(8,128)(2,1)S(1)}, bf16[1,128,320]{1,2,0:T(8,128)(2,1)S(1)}, u32[]{:S(2)}, u32[]{:S(2)}) collective-permute-start(bf16[1,128,320]{1,2,0:T(8,128)(2,1)S(1)} %get-tuple-element.48), channel_id=1, source_target_pairs={{16,0},{32,16},{48,32},{64,48},{80,64},{96,80},{112,96},{128,112},... | collective-permute-start | bytes 245768 | tf_op jit(solution)/shard_map/ppermute | solution.py:20
  19.7 1.9 collective-permute-start.1
  21.6 1.5 copy.30
  23.2 1.3 dynamic-slice.4
  25.4 1.1 fusion.5
  26.5 1.0 slice_dynamic-update-slice_fusion.5
  27.5 1.1 fusion.6
  28.6 1.1 fusion.7
  29.7 1.0 slice_dynamic-update-slice_fusion.4
  30.7 1.1 fusion.8
  31.8 1.1 fusion.9
  32.9 1.0 slice_dynamic-update-slice_fusion.3
  33.8 1.1 fusion.10
  34.9 8.4 %copy.29 = bf16[8,128,2880]{2,1,0:T(8,128)(2,1)} copy(bf16[8,128,2880]{1,2,0:T(8,128)(2,1)} %fusion.10) | data formatting | bytes 11796480 | tf_op jit(solution)/shard_map/concatenate | solution.py:48
  43.4 37.7 %all-gather.3.cloned.1.call-done = bf16[16,180,320]{2,1,0:T(8,128)(2,1)} async-done(((bf16[1,180,320]{2,1,0:T(8,128)(2,1)}), bf16[16,180,320]{2,1,0:T(8,128)(2,1)}) %all-gather.3.cloned.1.call-update) | async-done | bytes 1843216 | tf_op jit(solution)/shard_map/all_gather | solution.py:72
  81.1 2.8 reshape.78
  83.8 5.1 multiply_reduce_fusion.3
  89.1 71.5 %psum.63 = f32[32]{0:T(128)S(1)} all-reduce(f32[32]{0:T(128)S(1)} %reduce_sum.67), channel_id=1, replica_groups=mesh['tile'=32,'fsdp'=16] {'tile'}, use_global_device_ids=true, to_apply=%region_2.3 | all-reduce | flops 32 | bytes 256 | tf_op jit(solution)/shard_map/psum | solution.py:74
  161.4 62.7 %psum.64 = f32[32]{0:T(128)S(1)} all-reduce(f32[32]{0:T(128)S(1)} %reduce_sum.73), channel_id=1, replica_groups=mesh['tile'=32,'fsdp'=16] {'tile'}, use_global_device_ids=true, to_apply=%region_5.6 | all-reduce | flops 32 | bytes 256 | tf_op jit(solution)/shard_map/psum | solution.py:76
  224.3 3.5 multiply_reduce_fusion
  228.2 22.8 %all-reduce.5 = (f32[320]{0:T(512)S(1)}, f32[320]{0:T(512)S(1)}) all-reduce(f32[320]{0:T(512)S(1)} %get-tuple-element.32, f32[320]{0:T(512)S(1)} %get-tuple-element.35), channel_id=1, replica_groups=mesh['tile'=32,'fsdp'=16] {'fsdp'}, use_global_device_ids=true, to_apply=%region_15.16 | all-reduce | flops 640 | bytes 5120 | tf_op jit(solution)/shard_map/psum | solution.py:87
  251.0 70.8 %all-reduce.4 = (f32[32]{0:T(128)S(1)}, f32[32]{0:T(128)S(1)}, f32[320]{0:T(512)S(1)}, f32[320]{0:T(512)S(1)}) all-reduce(f32[32]{0:T(128)S(1)} %reduce_sum.93, f32[32]{0:T(128)S(1)} %reduce_sum.90, f32[320]{0:T(512)S(1)} %get-tuple-element.40, f32[320]{0:T(512)S(1)} %get-tuple-element.41), channel_id=1, replica_groups=mesh['tile'=32,'fsdp'=16] {'tile'}, use_global_device_ids=true, to_apply=%region_11.12 | all-reduce | flops 704 | bytes 5632 | tf_op jit(solution)/shard_map/psum | solution.py:85
  323.1 7.4 %convolution_convert_fusion = bf16[2880,320]{1,0:T(8,128)(2,1)} fusion(bf16[1024,2880]{1,0:T(8,128)(2,1)} %bitcast.60, bf16[1024,320]{0,1:T(8,128)(2,1)S(1)} %multiply_convert_fusion), kind=kOutput, calls=%fused_computation | convolution fusion | flops 1888358400 | bytes 8396800 | tf_op jit(solution)/shard_map/dot_general | solution.py:108
  331.3 32.9 %fusion = bf16[192,320]{1,0:T(8,128)(2,1)S(1)} fusion(bf16[2880,320]{1,0:T(8,128)(2,1)} %convolution_convert_fusion), kind=kCustom, calls=%all-reduce-scatter | all-reduce-scatter fusion | flops 983041 | bytes 1968128
  364.3 1.7 collective-permute-start.4
  366.7 5.5 %collective-permute-start.3 = (bf16[1,128,320]{1,2,0:T(8,128)(2,1)}, bf16[1,128,320]{1,2,0:T(8,128)(2,1)S(1)}, u32[]{:S(2)}, u32[]{:S(2)}) collective-permute-start(bf16[1,128,320]{1,2,0:T(8,128)(2,1)} %constant_dynamic-slice_fusion.1), channel_id=1, source_target_pairs={{0,16},{16,32},{32,48},{48,64},{64,80},{80,96},{96,112},{112,128},... | collective-permute-start | bytes 245768 | tf_op jit(solution)/shard_map/ppermute | solution.py:18
  372.2 5.3 collective-permute-start.2
  378.1 2.2 reshape.73
  380.3 1.8 reverse_bitcast_fusion
  382.2 2.5 copy.34
  384.6 1.2 copy.38
  385.9 0.9 copy.35
  387.0 1.1 fusion.11
  388.1 1.0 slice_dynamic-update-slice_fusion.2
  389.1 1.1 fusion.12
  390.2 1.1 fusion.13
  391.4 1.0 slice_dynamic-update-slice_fusion.1
  392.3 1.1 fusion.14
  393.4 1.1 fusion.15
  394.5 1.0 slice_dynamic-update-slice_fusion
  395.5 1.1 fusion.16
  396.6 8.6 %copy.33 = bf16[8,128,2880]{2,1,0:T(8,128)(2,1)} copy(bf16[8,128,2880]{1,2,0:T(8,128)(2,1)} %fusion.16) | data formatting | bytes 11796480 | tf_op jit(solution)/shard_map/concatenate | solution.py:48
  406.8 5.0 fusion.4
  411.9 0.9 copy.36
  412.8 115.3 %all-reduce.8.cloned.1.call-done = bf16[180,320]{1,0:T(8,128)(2,1)} async-done(((bf16[180,320]{1,0:T(8,128)(2,1)}), bf16[180,320]{1,0:T(8,128)(2,1)}) %all-reduce.8.cloned.1.call-update) | async-done | bytes 115216 | tf_op jit(solution)/shard_map/psum | solution.py:107
  528.1 2.0 divide_subtract_fusion
  (62 shorter events, 7.3 us)
Async XLA Ops:
  7.2 14.4 %copy-start.3 = (bf16[1,1,8,128,320]{3,4,2,1,0:T(8,128)(2,1)S(1)}, bf16[1,1,8,128,320]{3,4,2,1,0:T(8,128)(2,1)}, u32[]{:S(2)}) copy-start(bf16[1,1,8,128,320]{3,4,2,1,0:T(8,128)(2,1)} %param.10) | copy-start | bytes 1966084
  7.2 73.9 %all-gather.3.cloned.1.call-start = ((), (), s32[]{:S(2)}) async-start(), calls=%async_computation.1 | async-start | bytes 2402304 | tf_op jit(solution)/shard_map/all_gather | solution.py:72
  8.9 519.2 %all-reduce.8.cloned.1.call-start = ((), (), s32[]{:S(2)}) async-start(), calls=%async_computation | async-start | bytes 282624 | tf_op jit(solution)/shard_map/psum | solution.py:107
  10.9 14.3 %collective-permute-start = (bf16[1,128,320]{1,2,0:T(8,128)(2,1)S(1)}, bf16[1,128,320]{1,2,0:T(8,128)(2,1)S(1)}, u32[]{:S(2)}, u32[]{:S(2)}) collective-permute-start(bf16[1,128,320]{1,2,0:T(8,128)(2,1)S(1)} %get-tuple-element.48), channel_id=1, source_target_pairs={{16,0},{32,16},{48,32},{64,48},{80,64},{96,80},{112,96},{128,112},... | collective-permute-start | bytes 245768 | tf_op jit(solution)/shard_map/ppermute | solution.py:20
  19.7 5.5 %collective-permute-start.1 = (bf16[1,128,320]{1,2,0:T(8,128)(2,1)S(1)}, bf16[1,128,320]{1,2,0:T(8,128)(2,1)S(1)}, u32[]{:S(2)}, u32[]{:S(2)}) collective-permute-start(bf16[1,128,320]{1,2,0:T(8,128)(2,1)S(1)} %get-tuple-element.49), channel_id=1, source_target_pairs={{0,16},{16,32},{32,48},{48,64},{64,80},{80,96},{96,112},{112,128},... | collective-permute-start | bytes 245768 | tf_op jit(solution)/shard_map/ppermute | solution.py:18
  83.8 140.5 %copy-start.6 = (f32[320]{0:T(512)S(1)}, f32[320]{0:T(512)}, u32[]{:S(2)}) copy-start(f32[320]{0:T(512)} %param.12) | copy-start | bytes 3844
  83.8 140.5 %copy-start.7 = (f32[320]{0:T(512)S(1)}, f32[320]{0:T(512)}, u32[]{:S(2)}) copy-start(f32[320]{0:T(512)} %param.13) | copy-start | bytes 3844
  330.5 47.6 %copy-start = (bf16[16,180,320]{2,1,0:T(8,128)(2,1)S(1)}, bf16[16,180,320]{2,1,0:T(8,128)(2,1)}, u32[]{:S(2)}) copy-start(bf16[16,180,320]{2,1,0:T(8,128)(2,1)} %all-gather.3.cloned.1.call-done) | copy-start | bytes 5529604
  364.3 40.9 %collective-permute-start.4 = (bf16[180,320]{1,0:T(8,128)(2,1)S(1)}, bf16[180,320]{1,0:T(8,128)(2,1)S(1)}, u32[]{:S(2)}, u32[]{:S(2)}) collective-permute-start(bf16[180,320]{1,0:T(8,128)(2,1)S(1)} %slice.98), channel_id=1, source_target_pairs={{0,1},{1,2},{2,3},{3,4},{4,5},{5,6},{6,7},{7,8},{8,9},{9,10},{10,1... | collective-permute-start | bytes 345608
  366.7 20.1 %collective-permute-start.3 = (bf16[1,128,320]{1,2,0:T(8,128)(2,1)}, bf16[1,128,320]{1,2,0:T(8,128)(2,1)S(1)}, u32[]{:S(2)}, u32[]{:S(2)}) collective-permute-start(bf16[1,128,320]{1,2,0:T(8,128)(2,1)} %constant_dynamic-slice_fusion.1), channel_id=1, source_target_pairs={{0,16},{16,32},{32,48},{48,64},{64,80},{80,96},{96,112},{112,128},... | collective-permute-start | bytes 245768 | tf_op jit(solution)/shard_map/ppermute | solution.py:18
  372.2 14.6 %collective-permute-start.2 = (bf16[1,128,320]{1,2,0:T(8,128)(2,1)}, bf16[1,128,320]{1,2,0:T(8,128)(2,1)S(1)}, u32[]{:S(2)}, u32[]{:S(2)}) collective-permute-start(bf16[1,128,320]{1,2,0:T(8,128)(2,1)} %slice_bitcast_fusion), channel_id=1, source_target_pairs={{16,0},{32,16},{48,32},{64,48},{80,64},{96,80},{112,96},{128,112},... | collective-permute-start | bytes 245768 | tf_op jit(solution)/shard_map/ppermute | solution.py:20
  396.6 10.2 %copy-start.1 = (bf16[9,320,320]{2,1,0:T(8,128)(2,1)S(1)}, bf16[9,320,320]{2,1,0:T(8,128)(2,1)}, u32[]{:S(2)}) copy-start(bf16[9,320,320]{2,1,0:T(8,128)(2,1)} %copy.34) | copy-start | bytes 5529604
  411.7 116.4 %copy-start.2 = (f32[180,320]{1,0:T(8,128)S(1)}, f32[180,320]{1,0:T(8,128)}, u32[]{:S(2)}) copy-start(f32[180,320]{1,0:T(8,128)} %param.11) | copy-start | bytes 691204
  411.7 116.4 %copy-start.4 = (f32[180,320]{1,0:T(8,128)S(1)}, f32[180,320]{1,0:T(8,128)}, u32[]{:S(2)}) copy-start(f32[180,320]{1,0:T(8,128)} %param.14) | copy-start | bytes 691204
  411.8 116.4 %copy-start.5 = (f32[180,320]{1,0:T(8,128)S(1)}, f32[180,320]{1,0:T(8,128)}, u32[]{:S(2)}) copy-start(f32[180,320]{1,0:T(8,128)} %param.15) | copy-start | bytes 691204
Sparse Core Ops, SparseCore 0:
  10.7 70.3 all-gather.2
  406.9 121.1 all-reduce.7
